TPU v7x, 1024 devices: a whole 4x8x16 slice. The times are simulated.
1024 devices in a mesh: cuts: 4 (over x_lo, core), dp: 16 (over y, x_hi), tensor: 16 (over z).
Axes of the slice: x: 4 (x_hi: 2, x_lo: 2; x = x_hi * 2 + x_lo), y: 8, z: 16, core: 2. Of those that a mesh axis runs over, the one named last changes fastest.
Arguments:
- grad_out: bfloat16 [65536, 4096], P(('cuts', 'dp')), may hold values from -16 to 16
- attn_out: bfloat16 [65536, 4096], P(('cuts', 'dp'), 'tensor'), may hold values from -6 to 6
Outputs:
- grad_weight: float32 [4096, 4096], P(('cuts', 'dp'), 'tensor')
All inputs are finite; a program needn't handle non-finite values.
Results may differ from a plain program's by a relative error of at most 0.0003.
Values sent between devices are 32-bit elements; how exact they have to be, the bound alone decides.
No kernel may reach another device: no remote copies, remote signals or barrier semaphores. Data moves between devices by JAX's collectives and lax.ppermute only.
A program may use at most 32 MiB of HBM per device.

v0:
```python
import math

import jax
import jax.numpy as jnp
from jax import lax
from jax.sharding import PartitionSpec as P


def body(grad_out, attn_out):
    n_cuts = lax.axis_size("cuts")
    n_data = lax.axis_size("dp")
    tok_rows = grad_out.shape[0]
    factor = 1.0 / math.sqrt(float(tok_rows * n_cuts * n_data))
    summed = lax.psum_scatter(
        lax.dot_general(
            grad_out, attn_out, (((0,), (0,)), ((), ())), preferred_element_type=jnp.float32
        ),
        ("cuts", "dp"),
        scatter_dimension=0,
        tiled=True,
    )
    return summed * factor


def solution(mesh):
    placed = (P(("cuts", "dp"), None), P(("cuts", "dp"), "tensor"))
    return jax.shard_map(
        body, mesh=mesh, in_specs=placed, out_specs=P(("cuts", "dp"), "tensor"), check_vma=False
    )
```

profile of v0, /device:TPU:94, one launch (start us, length us, event | category | flops | bytes accessed | tf_op | source)
XLA Modules:
  0.0 344.5 jit_solution(14127374297905285080)
XLA Ops:
  6.5 0.0 copy-start
  6.5 0.0 reduce-scatter.2.cloned.1.call-start
  6.5 1.0 copy-done
  7.6 7.8 %fusion = f32[4096,256]{1,0:T(8,128)} fusion(bf16[1024,4096]{1,0:T(8,128)(2,1)} %param.2, bf16[1024,256]{1,0:T(8,128)(2,1)S(1)} %copy-done), kind=kOutput, calls=%fused_computation.1 | convolution fusion | flops 2147483648 | bytes 13107200 | tf_op jit(solution)/shard_map/dot_general | solution.py:15
  15.3 0.0 reduce-scatter.2.cloned.1.call-update
  15.4 320.8 %reduce-scatter.2.cloned.1.call-done = f32[64,256]{1,0:T(8,128)} async-done(((f32[4096,256]{1,0:T(8,128)}), f32[64,256]{1,0:T(8,128)}) %reduce-scatter.2.cloned.1.call-update) | async-done | bytes 65552 | tf_op jit(solution)/shard_map/reduce_scatter | solution.py:14
  336.2 1.5 broadcast_multiply_fusion
Async XLA Ops:
  6.5 1.0 copy-start
  6.5 329.6 %reduce-scatter.2.cloned.1.call-start = ((), (), s32[]{:S(2)}) async-start(), calls=%async_computation.1 | async-start | bytes 4259840 | tf_op jit(solution)/shard_map/reduce_scatter | solution.py:14
Sparse Core Ops, SparseCore 0:
  15.5 320.6 reduce-scatter.1
where the time goes:
time: 345 us; the launch traced here: 344 us
  waiting for transfers between devices  321 us (93%)
  between operations  13.4 us (4%)
  matrix products  7.77 us (2%)
    reduce_scatter x1, waiting for transfers between devices, body(): lax.psum_scatter(lax.dot_general(grad_out, attn_out, (((0,), (0,)), ((),...  321 us
    dot_general x1, matrix products, body(): lax.dot_general(grad_out, attn_out, (((0,), (0,)), ((), ())), preferred_e...  7.77 us
  transfers between devices with their start and end apart: 1, of which 1 were waited for; matrix products, arithmetic and copies ran while one was open for 0% of the time, Pallas kernels for 0%

commit v1 on v0

v1 whole, which is shorter than its diff:
```python
import math

import jax
import jax.numpy as jnp
from jax import lax
from jax.sharding import Mesh, PartitionSpec as P

CHIP_ORDER = ("y", "xh", "xl", "core")
OWNERS = ("xl", "core", "y", "xh")


def body(grad_out, attn_out):
    sizes = {axis: lax.axis_size(axis) for axis in OWNERS}
    shards = math.prod(sizes.values())
    factor = 1.0 / math.sqrt(float(grad_out.shape[0] * shards))
    partial = lax.dot_general(
        grad_out, attn_out, (((0,), (0,)), ((), ())), preferred_element_type=jnp.float32
    )
    rows, columns = partial.shape[0] // shards, partial.shape[1]
    blocks = partial.reshape(tuple(sizes[axis] for axis in OWNERS) + (rows, columns))
    order = tuple(OWNERS.index(axis) for axis in CHIP_ORDER)
    blocks = blocks.transpose(order + (4, 5)).reshape(shards * rows, columns)
    summed = lax.psum_scatter(blocks, CHIP_ORDER, scatter_dimension=0, tiled=True)
    return summed * factor


def solution(mesh):
    cuts, dp, tensor = mesh.devices.shape
    parts = mesh.devices.reshape(2, cuts // 2, dp // 2, 2, tensor)
    chips = Mesh(parts, OWNERS + ("z",))
    placed = (P(OWNERS, None), P(OWNERS, "z"))
    return jax.shard_map(body, mesh=chips, in_specs=placed, out_specs=P(OWNERS, "z"), check_vma=False)
```

time: 345 us -> 201 us (0.58)
  the two profiles are of different devices: /device:TPU:94 before, /device:TPU:16 now
where the time goes in v1:
time: 201 us; the launch traced here: 200 us
  waiting for transfers between devices  177 us (88%)
  between operations  13.4 us (7%)
  matrix products  5.84 us (3%)
  local copies, waits for them, and re-layouts  3.27 us (2%)
    reduce_scatter x1, waiting for transfers between devices, body(): lax.psum_scatter(blocks, CHIP_ORDER, scatter_dimension=0, tiled=True)  176 us
    dot_general x1, matrix products, body(): lax.dot_general(grad_out, attn_out, (((0,), (0,)), ((), ())), preferred_e...  5.84 us
  transfers between devices with their start and end apart: 1, of which 1 were waited for; matrix products, arithmetic and copies ran while one was open for 0% of the time, Pallas kernels for 0%

profile of v1, /device:TPU:16, one launch (start us, length us, event | category | flops | bytes accessed | tf_op | source)
XLA Modules:
  0.0 200.5 jit_solution(2225912151463777208)
XLA Ops:
  6.5 0.0 copy-start
  6.5 0.0 reduce-scatter.2.cloned.1.call-start
  6.5 1.0 copy-done
  7.6 5.8 %fusion = f32[4096,256]{1,0:T(8,128)S(1)} fusion(bf16[1024,4096]{1,0:T(8,128)(2,1)} %param.2, bf16[1024,256]{1,0:T(8,128)(2,1)S(1)} %copy-done), kind=kOutput, calls=%fused_computation.1 | convolution fusion | flops 2147483648 | bytes 13107200 | tf_op jit(solution)/shard_map/dot_general | solution.py:16
  13.4 2.2 %copy.3 = f32[8,2,2,2,64,256]{5,4,3,2,1,0:T(8,128)} copy(f32[8,2,2,2,64,256]{5,4,1,0,3,2:T(8,128)S(1)} %bitcast.7) | data formatting | bytes 8388608 | tf_op jit(solution)/shard_map/transpose | solution.py:22
  15.7 0.0 reduce-scatter.2.cloned.1.call-update
  15.7 176.5 %reduce-scatter.2.cloned.1.call-done = f32[64,256]{1,0:T(8,128)} async-done(((f32[4096,256]{1,0:T(8,128)}), f32[64,256]{1,0:T(8,128)}) %reduce-scatter.2.cloned.1.call-update) | async-done | bytes 65552 | tf_op jit(solution)/shard_map/reduce_scatter | solution.py:23
  192.2 1.5 broadcast_multiply_fusion
Async XLA Ops:
  6.5 1.0 copy-start
  6.5 185.6 %reduce-scatter.2.cloned.1.call-start = ((), (), s32[]{:S(2)}) async-start(), calls=%async_computation.1 | async-start | bytes 4259840 | tf_op jit(solution)/shard_map/reduce_scatter | solution.py:23
Sparse Core Ops, SparseCore 0:
  15.8 176.3 reduce-scatter.1
